TPU v7x, 32 devices: a whole 2x2x4 slice. The times are simulated.
32 devices in a mesh: groups: 2 (over x), img: 16 (over z, y, core).
Axes of the slice: x: 2, y: 2, z: 4, core: 2. Of those that a mesh axis runs over, the one named last changes fastest.
Arguments:
- tokens: bfloat16 [64, 128, 768], P(('groups', 'img')), parts along dimension 0, may hold values from -6 to 6
- partners: int32 [64, 8], P(('groups', 'img')), parts along dimension 0, may hold values from 0 to 31, as said below
- counts: int32 [64], P(('groups', 'img')), parts along dimension 0, may hold values from 4 to 8, as said below
- gain_query: float32 [768], replicated, may hold values from 0.5 to 12
- gain_memory: float32 [768], replicated, may hold values from 0.25 to 1.75
- w_query: bfloat16 [768, 768], replicated, may hold values from -0.21875 to 0.21875
- w_key: bfloat16 [768, 768], replicated, may hold values from -0.21875 to 0.21875
- w_value: bfloat16 [768, 768], replicated, may hold values from -0.21875 to 0.21875
- w_out: bfloat16 [768, 768], replicated, may hold values from -0.21875 to 0.21875
Outputs:
- mixed: bfloat16 [64, 128, 768], P(('groups', 'img')), parts along dimension 0
There are 2 independent parts, one for each index of `groups`. A program takes and returns all parts, laid end to end along the dimension named above; an argument that names none is the same for every part. Nothing has to cross between parts.
Inputs may be any that keep to these rules, and one draw needn't show every extreme that they name: No image is its own partner. Over the first counts[a] partners of all images a of one device (image i belongs to device i // 2), at most 1 lie with any one device, and every device reaches 1 with some device. `counts`: every device owns an image with 8 pairs.
All inputs are finite; a program needn't handle non-finite values.
Results may differ from a plain program's by a relative error of at most 0.0067.
Values may be sent and summed in bfloat16 or wider, within the bound.
A program may use at most 128 MiB of HBM per device.

v0:
```python
import jax
import jax.numpy as jnp
from jax import lax
from jax.sharding import PartitionSpec as P

HEADS = 12
HEAD_DIM = 64


def normalize(rows, gain):
    rows = rows.astype(jnp.float32)
    center = rows - jnp.mean(rows, axis=-1, keepdims=True)
    spread = jnp.mean(center * center, axis=-1, keepdims=True)
    return center * lax.rsqrt(spread + 1e-06) * gain


def slot_table(partner_rows, count_rows, own_count, peer_count):
    width = partner_rows.shape[1]
    live = (jnp.arange(width, dtype=jnp.int32)[None, :] < count_rows[:, None]).reshape(-1)
    owner = (partner_rows // own_count).reshape(-1)
    onehot = (
        (owner[:, None] == jnp.arange(peer_count, dtype=jnp.int32)[None, :]) & live[:, None]
    ).astype(jnp.int32)
    before = jnp.cumsum(onehot, axis=0) - onehot
    slot = jnp.sum(before * onehot, axis=1)
    return (owner, slot, live)


def shards(tokens, partners, counts, gain_query, gain_memory, w_query, w_key, w_value, w_out):
    own_count, tok_rows, width = tokens.shape
    listed = partners.shape[1]
    peer_count = lax.axis_size("img")
    slot_cap = (own_count * listed + peer_count - 1) // peer_count
    first_image = lax.axis_index("img") * own_count
    rows = tokens.reshape(own_count * tok_rows, width)
    normed_query = normalize(rows, gain_query).astype(jnp.bfloat16)
    normed_memory = normalize(rows, gain_memory).astype(jnp.bfloat16)
    queries = jnp.dot(normed_query, w_query, preferred_element_type=jnp.float32).astype(
        jnp.bfloat16
    )
    queries = queries.reshape(own_count, tok_rows, HEADS, HEAD_DIM)
    my_owner, my_slot, my_live = slot_table(partners, counts, own_count, peer_count)
    target = jnp.where(my_live, my_owner, peer_count)
    request = (
        jnp.full((peer_count, slot_cap), -1, jnp.int32)
        .at[target, my_slot]
        .set(partners.reshape(-1), mode="drop")
    )
    wanted = lax.all_to_all(request, "img", split_axis=0, concat_axis=0, tiled=True)
    used = wanted >= 0
    local_index = jnp.clip(wanted - first_image, 0, own_count - 1)
    pick = jnp.clip(my_owner, 0, peer_count - 1) * slot_cap + jnp.clip(my_slot, 0, slot_cap - 1)
    picked = normed_memory.reshape(own_count, tok_rows, width)[local_index]
    got_memory = lax.all_to_all(
        jnp.where(used[:, :, None, None], picked, jnp.zeros_like(picked)),
        "img",
        split_axis=0,
        concat_axis=0,
        tiled=True,
    )
    pair_memory = got_memory.reshape(peer_count * slot_cap, tok_rows, width)[pick].reshape(
        -1, width
    )
    pair_keys = jnp.dot(pair_memory, w_key, preferred_element_type=jnp.float32).astype(jnp.bfloat16)
    pair_values = jnp.dot(pair_memory, w_value, preferred_element_type=jnp.float32).astype(
        jnp.bfloat16
    )
    pair_keys = pair_keys.reshape(own_count, listed, tok_rows, HEADS, HEAD_DIM)
    pair_values = pair_values.reshape(own_count, listed, tok_rows, HEADS, HEAD_DIM)
    scale = 1.0 / HEAD_DIM**0.5

    def one_image(item):
        query_rows, key_rows, value_rows, count = item
        scores = (
            jnp.einsum("qhd,kjhd->hkqj", query_rows, key_rows, preferred_element_type=jnp.float32)
            * scale
        )
        probs = jax.nn.softmax(scores, axis=-1).astype(jnp.bfloat16)
        pair_context = jnp.einsum(
            "hkqj,kjhd->kqhd", probs, value_rows, preferred_element_type=jnp.float32
        )
        live = jnp.arange(listed, dtype=jnp.int32) < count
        total = jnp.sum(
            jnp.where(live[:, None, None, None], pair_context, jnp.float32(0.0)), axis=0
        )
        return total.reshape(tok_rows, width) / count.astype(jnp.float32)

    context = lax.map(one_image, (queries, pair_keys, pair_values, counts)).astype(jnp.bfloat16)
    mixed = rows.astype(jnp.float32) + jnp.dot(
        context.reshape(-1, width), w_out, preferred_element_type=jnp.float32
    )
    return mixed.astype(jnp.bfloat16).reshape(own_count, tok_rows, width)


def solution(mesh):
    placed = (
        P(("groups", "img"), None, None),
        P(("groups", "img"), None),
        P(("groups", "img")),
        P(),
        P(),
        P(),
        P(),
        P(),
        P(),
    )
    return jax.shard_map(
        shards,
        mesh=mesh,
        in_specs=placed,
        out_specs=P(("groups", "img"), None, None),
        check_vma=False,
    )
```

profile of v0, /device:TPU:13, one launch (start us, length us, event | category | flops | bytes accessed | tf_op | source)
XLA Modules:
  0.0 160.1 jit_solution(5718504146963567102)
XLA Ops:
  0.0 0.8 broadcast_clamp_fusion
  0.8 0.1 eq.15
  0.9 0.7 iota_compare_fusion.2
  1.6 0.7 broadcast_select_fusion
  2.3 0.8 reshape.260
  3.1 0.1 lt.81
  3.3 0.2 select_reduce_fusion.1
  3.5 0.1 select_n.74
  3.6 0.6 scatter_custom_fusion
  4.3 0.7 copy.39
  5.0 6.6 %all-to-all-start = ((s32[16,1,1]{2,1,0:T(1,128)}), s32[16,1,1]{2,1,0:T(1,128)S(1)}, u32[]{:S(2)}, u32[]{:S(2)}) async-start(s32[16,1,1]{2,1,0:T(1,128)} %copy.39), calls=%async_computation | async-start | bytes 16384 | tf_op jit(solution)/shard_map/all_to_all | solution.py:49
  11.5 1.1 convert_reduce_fusion
  12.6 1.2 multiply_reduce_fusion
  13.9 1.2 multiply_convert_fusion
  15.1 0.1 all-to-all-done
  15.2 0.4 fusion.20
  15.6 2.5 %gather_fusion = bf16[16,128,768]{2,1,0:T(8,128)(2,1)} fusion(bf16[2,128,768]{2,1,0:T(8,128)(2,1)S(1)} %multiply_convert_fusion, s32[1024]{0:T(1024)S(1)} %pad_clamp_fusion.1), kind=kCustom, calls=%fused_computation | custom fusion | bytes 6291520 | tf_op jit(solution)/shard_map/gather | solution.py:53
  18.1 0.4 compare_reduce_fusion
  18.5 3.9 %bitcast_select_fusion = bf16[16,1,128,768]{3,2,1,0:T(8,128)(2,1)} fusion(bf16[16,128,768]{2,1,0:T(8,128)(2,1)} %gather_fusion, pred[16]{0:T(512)(128)(4,1)S(1)} %compare_reduce_fusion), kind=kLoop, calls=%fused_computation.28 | loop fusion | flops 1572864 | bytes 6291472 | tf_op jit(solution)/shard_map/jit(_where)/select_n | solution.py:55
  22.3 7.1 %all-to-all-start.1 = ((bf16[16,1,128,768]{3,2,1,0:T(8,128)(2,1)}), bf16[16,1,128,768]{3,2,1,0:T(8,128)(2,1)}, u32[]{:S(2)}, u32[]{:S(2)}) async-start(bf16[16,1,128,768]{3,2,1,0:T(8,128)(2,1)} %bitcast_select_fusion), calls=%async_computation.1 | async-start | bytes 6291456 | tf_op jit(solution)/shard_map/all_to_all | solution.py:54
  29.4 0.2 fusion.19
  29.7 0.5 convolution_convert_fusion.2
  30.2 0.2 copy.42
  30.3 0.1 reshape.234
  30.5 68.9 %all-to-all-done.1 = bf16[16,1,128,768]{3,2,1,0:T(8,128)(2,1)} async-done(((bf16[16,1,128,768]{3,2,1,0:T(8,128)(2,1)}), bf16[16,1,128,768]{3,2,1,0:T(8,128)(2,1)}, u32[]{:S(2)}, u32[]{:S(2)}) %all-to-all-start.1) | async-done | bytes 3145760 | tf_op jit(solution)/shard_map/all_to_all | solution.py:54
  99.4 4.3 %gather_fusion.1 = bf16[16,128,768]{2,1,0:T(8,128)(2,1)} fusion(bf16[16,128,768]{2,1,0:T(8,128)(2,1)} %bitcast.14, s32[1024]{0:T(1024)S(1)} %pad_clamp_fusion), kind=kCustom, calls=%fused_computation.1 | custom fusion | bytes 6291520 | tf_op jit(solution)/shard_map/gather | solution.py:61
  103.8 6.2 %convolution_convert_fusion.1 = bf16[2048,768]{1,0:T(8,128)(2,1)} fusion(bf16[2048,768]{1,0:T(8,128)(2,1)} %bitcast.100, bf16[768,768]{1,0:T(8,128)(2,1)S(1)} %copy-done), kind=kOutput, calls=%fused_computation.27 | convolution fusion | flops 2417491968 | bytes 7471104 | tf_op jit(solution)/shard_map/dot_general | solution.py:65
  110.0 4.8 %copy.40 = bf16[2048,768]{0,1:T(8,128)(2,1)} copy(bf16[2048,768]{1,0:T(8,128)(2,1)} %convolution_convert_fusion.1) | data formatting | bytes 6291456 | tf_op jit(solution)/shard_map/convert_element_type | solution.py:65
  114.7 4.7 %copy.56 = bf16[96,8,16,128]{3,2,1,0:T(8,128)(2,1)} copy(bf16[96,8,16,128]{3,1,2,0:T(8,128)(2,1)} %bitcast.97) | data formatting | bytes 6291456
  119.5 4.0 %convolution_convert_fusion = bf16[2048,768]{1,0:T(8,128)(2,1)} fusion(bf16[2048,768]{1,0:T(8,128)(2,1)S(1)} %bitcast.101, bf16[768,768]{1,0:T(8,128)(2,1)S(1)} %copy-done.7), kind=kOutput, calls=%fused_computation.26 | convolution fusion | flops 2417491968 | bytes 7471104 | tf_op jit(solution)/shard_map/dot_general | solution.py:64
  123.4 4.8 %copy.41 = bf16[2048,768]{0,1:T(8,128)(2,1)} copy(bf16[2048,768]{1,0:T(8,128)(2,1)} %convolution_convert_fusion) | data formatting | bytes 6291456 | tf_op jit(solution)/shard_map/convert_element_type | solution.py:64
  128.2 4.7 %copy.57 = bf16[96,8,16,128]{3,2,1,0:T(8,128)(2,1)} copy(bf16[96,8,16,128]{3,1,2,0:T(8,128)(2,1)} %bitcast.98) | data formatting | bytes 6291456
  132.9 24.7 %while.10 = (s32[]{:T(128)}, bf16[2,128,768]{2,1,0:T(8,128)(2,1)S(1)}, s32[2]{0:T(128)S(1)}, bf16[2,8,128,12,64]{2,1,0,4,3:T(8,128)(2,1)}, bf16[2,8,128,12,64]{2...) while((s32[]{:T(128)}, bf16[2,128,768]{2,1,0:T(8,128)(2,1)S(1)}, s32[2]{0:T(128)S(1)}, ...), condition=%wide.region_9.10_spmd, body=%wide.region_5.9_spmd.sunk | while | flops 413761664 | bytes 36667524 | solution.py:88
  132.9 2.2 %constant_dynamic-slice_fusion.3 = (bf16[1,8,128,12,64]{2,1,0,4,3:T(8,128)(2,1)S(1)}, bf16[1,8,128,12,64]{2,1,0,4,3:T(8,128)(2,1)S(1)}) fusion(bf16[2,8,128,12,64]{2,1,0,4,3:T(8,128)(2,1)} %get-tuple-element.155, s32[]{:T(128)} %get-tuple-element.144, bf16[2,8,128,12,64]{2,1,0,4,3:T(8,128)(2,1)} %get-tuple-element.154), kind=kLoop, calls=%fused_computation.22.clone.1 | loop fusion | bytes 6291460 | tf_op jit(solution)/shard_map/while/body/jit(dynamic_index_in_dim)/dynamic_slice | solution.py:88
  135.0 1.1 fusion.46
  136.1 5.9 %fusion.47 = (f32[12,8,128]{2,1,0:T(8,128)S(1)}, f32[12,8,128,128]{2,3,1,0:T(8,128)S(1)}) fusion(f32[12,8,128,128]{3,2,1,0:T(8,128)S(1)} %fusion.46), kind=kOutput, calls=%fused_computation.70.clone.1 | output fusion | flops 6291583 | bytes 12632064 | tf_op jit(solution)/shard_map/while/body/eval_jaxpr/sub | solution.py:78
  142.0 0.6 dynamic_slice.26
  142.6 0.6 iota_compare_fusion.4
  143.3 1.0 select_reduce_fusion.3
  145.0 0.1 copy.73
  145.2 2.2 %constant_dynamic-slice_fusion.3 = (bf16[1,8,128,12,64]{2,1,0,4,3:T(8,128)(2,1)S(1)}, bf16[1,8,128,12,64]{2,1,0,4,3:T(8,128)(2,1)S(1)}) fusion(bf16[2,8,128,12,64]{2,1,0,4,3:T(8,128)(2,1)} %get-tuple-element.155, s32[]{:T(128)} %get-tuple-element.144, bf16[2,8,128,12,64]{2,1,0,4,3:T(8,128)(2,1)} %get-tuple-element.154), kind=kLoop, calls=%fused_computation.22.clone.1 | loop fusion | bytes 6291460 | tf_op jit(solution)/shard_map/while/body/jit(dynamic_index_in_dim)/dynamic_slice | solution.py:88
  147.4 1.1 fusion.46
  148.5 5.9 %fusion.47 = (f32[12,8,128]{2,1,0:T(8,128)S(1)}, f32[12,8,128,128]{2,3,1,0:T(8,128)S(1)}) fusion(f32[12,8,128,128]{3,2,1,0:T(8,128)S(1)} %fusion.46), kind=kOutput, calls=%fused_computation.70.clone.1 | output fusion | flops 6291583 | bytes 12632064 | tf_op jit(solution)/shard_map/while/body/eval_jaxpr/sub | solution.py:78
  154.4 0.6 dynamic_slice.26
  155.0 0.6 iota_compare_fusion.4
  155.7 1.0 select_reduce_fusion.3
  157.4 0.1 copy.73
  157.6 2.5 %fusion.16 = bf16[256,768]{1,0:T(8,128)(2,1)} fusion(bf16[256,768]{1,0:T(8,128)(2,1)S(1)} %bitcast.102, bf16[768,768]{1,0:T(8,128)(2,1)} %param.19, bf16[256,768]{1,0:T(8,128)(2,1)S(1)} %bitcast.99), kind=kOutput, calls=%fused_computation.30 | convolution fusion | flops 302579712 | bytes 2359296 | tf_op jit(solution)/shard_map/dot_general | solution.py:89
  (30 shorter events, 0.5 us)
Async XLA Ops:
  0.0 103.8 %copy-start = (bf16[768,768]{1,0:T(8,128)(2,1)S(1)}, bf16[768,768]{1,0:T(8,128)(2,1)}, u32[]{:S(2)}) copy-start(bf16[768,768]{1,0:T(8,128)(2,1)} %param.18) | copy-start | bytes 3538948
  5.0 10.3 %all-to-all-start = ((s32[16,1,1]{2,1,0:T(1,128)}), s32[16,1,1]{2,1,0:T(1,128)S(1)}, u32[]{:S(2)}, u32[]{:S(2)}) async-start(s32[16,1,1]{2,1,0:T(1,128)} %copy.39), calls=%async_computation | async-start | bytes 16384 | tf_op jit(solution)/shard_map/all_to_all | solution.py:49
  22.3 7.1 %copy-start.1 = (bf16[2,128,768]{2,1,0:T(8,128)(2,1)S(1)}, bf16[2,128,768]{2,1,0:T(8,128)(2,1)}, u32[]{:S(2)}) copy-start(bf16[2,128,768]{2,1,0:T(8,128)(2,1)} %param.11) | copy-start | bytes 1179652
  22.3 7.1 %copy-start.5 = (f32[768]{0:T(1024)S(1)}, f32[768]{0:T(1024)}, u32[]{:S(2)}) copy-start(f32[768]{0:T(1024)} %param.14) | copy-start | bytes 9220
  22.3 7.3 %copy-start.3 = (bf16[768,768]{1,0:T(8,128)(2,1)S(1)}, bf16[768,768]{1,0:T(8,128)(2,1)}, u32[]{:S(2)}) copy-start(bf16[768,768]{1,0:T(8,128)(2,1)} %param.16) | copy-start | bytes 3538948
  22.3 77.1 %all-to-all-start.1 = ((bf16[16,1,128,768]{3,2,1,0:T(8,128)(2,1)}), bf16[16,1,128,768]{3,2,1,0:T(8,128)(2,1)}, u32[]{:S(2)}, u32[]{:S(2)}) async-start(bf16[16,1,128,768]{3,2,1,0:T(8,128)(2,1)} %bitcast_select_fusion), calls=%async_computation.1 | async-start | bytes 6291456 | tf_op jit(solution)/shard_map/all_to_all | solution.py:54
  114.7 4.7 %copy-start.2 = (bf16[16,128,768]{2,1,0:T(8,128)(2,1)S(1)}, bf16[16,128,768]{2,1,0:T(8,128)(2,1)}, u32[]{:S(2)}) copy-start(bf16[16,128,768]{2,1,0:T(8,128)(2,1)} %gather_fusion.1) | copy-start | bytes 9437188
  114.7 4.7 %copy-start.7 = (bf16[768,768]{1,0:T(8,128)(2,1)S(1)}, bf16[768,768]{1,0:T(8,128)(2,1)}, u32[]{:S(2)}) copy-start(bf16[768,768]{1,0:T(8,128)(2,1)} %param.17) | copy-start | bytes 3538948
  128.2 4.7 %copy-start.4 = (bf16[2,128,768]{2,1,0:T(8,128)(2,1)S(1)}, bf16[2,128,768]{2,1,0:T(8,128)(2,1)}, u32[]{:S(2)}) copy-start(bf16[2,128,768]{2,1,0:T(8,128)(2,1)} %custom-call.4) | copy-start | bytes 1179652
  128.2 4.7 %copy-start.6 = (s32[2]{0:T(128)S(1)}, s32[2]{0:T(128)}, u32[]{:S(2)}) copy-start(s32[2]{0:T(128)} %param.13) | copy-start | bytes 28
where the time goes:
time: 161 us; the launch traced here: 160 us
  waiting for transfers between devices  69 us (43%)
  local copies, waits for them, and re-layouts  34.3 us (21%)
  other arithmetic  24.2 us (15%)
  matrix products  17.4 us (11%)
  starting transfers between devices  13.6 us (8%)
    all_to_all x1, waiting for transfers between devices, shards(): lax.all_to_all(jnp.where(used[:, :, None, None], picked, jnp.zeros_like(p...  68.9 us
    sub x2, other arithmetic, one_image(): probs = jax.nn.softmax(scores, axis=-1).astype(jnp.bfloat16)  11.8 us
    unnamed x18, local copies, waits for them, and re-layouts  9.42 us
    all_to_all x1, starting transfers between devices, shards(): lax.all_to_all(jnp.where(used[:, :, None, None], picked, jnp.zeros_like(p...  7.08 us
    all_to_all x1, starting transfers between devices, shards(): lax.all_to_all(request, 'img', split_axis=0, concat_axis=0, tiled=True)  6.55 us
    dot_general x1, matrix products, shards(): jnp.dot(pair_memory, w_value, preferred_element_type=jnp.float32)  6.18 us
    dynamic_slice x4, local copies, waits for them, and re-layouts, shards(): lax.map(one_image, (queries, pair_keys, pair_values, counts))  5.53 us
    convert_element_type x1, local copies, waits for them, and re-layouts, shards(): jnp.dot(pair_memory, w_value, preferred_element_type=jnp.float32)  4.76 us
  transfers between devices with their start and end apart: 2, of which 2 were waited for; matrix products, arithmetic and copies ran while one was open for 3% of the time, Pallas kernels for 0%

commit v1 on v0

--- a/solution.py
+++ b/solution.py
@@ -1,10 +1,16 @@
+import functools
+
 import jax
 import jax.numpy as jnp
 from jax import lax
+from jax.experimental import pallas as pl
+from jax.experimental.pallas import tpu as pltpu
 from jax.sharding import PartitionSpec as P
 
 HEADS = 12
 HEAD_DIM = 64
+LAYERS = 4
+UP, DOWN, TWIN, SIBLING = 0, 1, 2, 3
 
 
 def normalize(rows, gain):
@@ -26,7 +32,7 @@
     return (owner, slot, live)
 
 
-def shards(tokens, partners, counts, gain_query, gain_memory, w_query, w_key, w_value, w_out):
+def exchange(tokens, partners, counts, gain_query, gain_memory, w_query, w_key, w_value, w_out):
     own_count, tok_rows, width = tokens.shape
     listed = partners.shape[1]
     peer_count = lax.axis_size("img")
@@ -92,6 +98,260 @@
     return mixed.astype(jnp.bfloat16).reshape(own_count, tok_rows, width)
 
 
+def layer_at(step, z):
+    first = (LAYERS - 1 - step) // (LAYERS - 1)
+    last = step // (LAYERS - 1)
+    third = step // 2 * (1 - last)
+    second = 1 - first - third - last
+    return (
+        first * z
+        + second * (1 + z % 2)
+        + third * ((2 + 3 * z) % 5)
+        + last * (LAYERS - 1) * (1 - z // 2)
+    )
+
+
+def fused_kernel(
+    tokens_ref,
+    partners_ref,
+    counts_ref,
+    gain_query_ref,
+    gain_memory_ref,
+    w_query_ref,
+    w_key_ref,
+    w_value_ref,
+    w_out_ref,
+    mixed_ref,
+    held,
+    block_q,
+    w_turned,
+    keys_ref,
+    values_ref,
+    total,
+    send_sem,
+    recv_sem,
+):
+    own_count, tok_rows, width = tokens_ref.shape
+    listed = partners_ref.shape[1]
+    pairs = width // 128
+    me = lax.axis_index("img")
+    core, y, z = me % 2, me // 2 % 2, me // 4
+
+    def index(layer, row, lane):
+        return layer * 4 + row * 2 + lane
+
+    def to(peer):
+        return {"img": peer}
+
+    up, down = index(z + 1, y, core), index(z - 1, y, core)
+    twin, sibling = index(z, 1 - y, core), index(z, y, 1 - core)
+
+    def copy(owner, way, peer):
+        return pltpu.make_async_remote_copy(
+            src_ref=held.at[owner],
+            dst_ref=held.at[owner],
+            send_sem=send_sem.at[owner, way],
+            recv_sem=recv_sem.at[owner],
+            device_id=to(peer),
+            device_id_type=pl.DeviceIdType.MESH,
+        )
+
+    def arrived(owner):
+        copy(owner, SIBLING, sibling).wait_recv()
+
+    barrier = pltpu.get_barrier_semaphore()
+
+    def greet(peer):
+        pl.semaphore_signal(
+            barrier, inc=1, device_id=to(peer), device_id_type=pl.DeviceIdType.MESH
+        )
+
+    greet(sibling)
+    greet(twin)
+
+    @pl.when(z < LAYERS - 1)
+    def _():
+        greet(up)
+
+    @pl.when(z > 0)
+    def _():
+        greet(down)
+
+    rows = tokens_ref[...].reshape(own_count * tok_rows, width).astype(jnp.float32)
+    center = rows - jnp.mean(rows, axis=-1, keepdims=True)
+    spread = jnp.mean(center * center, axis=-1, keepdims=True)
+    unit = center * lax.rsqrt(spread + 1e-06)
+    held[me] = (
+        (unit * gain_memory_ref[...]).astype(jnp.bfloat16).reshape(own_count, tok_rows, width)
+    )
+
+    pl.semaphore_wait(barrier, 3 + (z + LAYERS - 2) // (LAYERS - 1) - z // (LAYERS - 1))
+
+    def pass_on(layer, act):
+        owner = index(layer, y, core)
+        act(owner, TWIN, twin)
+
+        @pl.when((layer <= z) & (z < LAYERS - 1))
+        def _():
+            act(owner, UP, up)
+
+        @pl.when((layer >= z) & (z > 0))
+        def _():
+            act(owner, DOWN, down)
+
+        act(owner, SIBLING, sibling)
+
+    def begin(owner, way, peer):
+        copy(owner, way, peer).start()
+
+    def finish(owner, way, peer):
+        copy(owner, way, peer).wait_send()
+
+    pass_on(z, begin)
+
+    normed_query = (unit * gain_query_ref[...]).astype(jnp.bfloat16)
+    w_turned[...] = w_query_ref[...].T
+    queries = lax.dot_general(
+        w_turned[...], normed_query, (((1,), (1,)), ((), ())), preferred_element_type=jnp.float32
+    ).astype(jnp.bfloat16) * jnp.bfloat16(1.0 / HEAD_DIM**0.5)
+    blank = jnp.zeros((HEAD_DIM, tok_rows), jnp.bfloat16)
+    for image in range(own_count):
+        for pair in range(pairs):
+            both = queries[
+                pair * 128 : (pair + 1) * 128, image * tok_rows : (image + 1) * tok_rows
+            ]
+            upper = jnp.concatenate([both[:HEAD_DIM], blank], axis=1)
+            lower = jnp.concatenate([blank, both[HEAD_DIM:]], axis=1)
+            block_q[image, pair] = jnp.concatenate([upper, lower], axis=0)
+    w_turned[...] = w_value_ref[...].T
+    total[...] = jnp.zeros_like(total)
+
+    def pair_of(owner):
+        which, within = jnp.int32(0), jnp.int32(0)
+        weights = []
+        for image in range(own_count):
+            found = jnp.int32(0)
+            for k in range(listed):
+                partner = partners_ref[image, k]
+                hit = ((partner // own_count == owner) & (k < counts_ref[image])).astype(jnp.int32)
+                found = found + hit
+                within = within + hit * (partner % own_count)
+            which = which + image * found
+            weights.append(found.astype(jnp.float32))
+        return which, within, weights
+
+    def attend(layer, row):
+        owners = [index(layer, row, lane) for lane in range(2)]
+        found = [pair_of(owner) for owner in owners]
+        memory = jnp.concatenate(
+            [
+                jnp.where(within == 0, held[owner, 0], held[owner, 1])
+                for owner, (_, within, _) in zip(owners, found)
+            ],
+            axis=0,
+        )
+        keys_ref[...] = jnp.dot(
+            memory, w_key_ref[...], preferred_element_type=jnp.float32
+        ).astype(jnp.bfloat16)
+        values_ref[...] = lax.dot_general(
+            w_turned[...], memory, (((1,), (1,)), ((), ())), preferred_element_type=jnp.float32
+        ).astype(jnp.bfloat16)
+        for lane, (which, _, weights) in enumerate(found):
+            span = slice(lane * tok_rows, (lane + 1) * tok_rows)
+            for pair in range(pairs):
+                part = slice(pair * 128, (pair + 1) * 128)
+                scores = jnp.dot(
+                    keys_ref[span, part], block_q[which, pair], preferred_element_type=jnp.float32
+                )
+                grown = jnp.exp(scores - jnp.max(scores, axis=0, keepdims=True))
+                share = 1.0 / jnp.sum(grown, axis=0, keepdims=True)
+                probs = (grown * share).astype(jnp.bfloat16)
+                mixed = jnp.dot(values_ref[part, span], probs, preferred_element_type=jnp.float32)
+                for head in range(2):
+                    inner = slice(head * HEAD_DIM, (head + 1) * HEAD_DIM)
+                    outer = slice(pair * 128 + head * HEAD_DIM, pair * 128 + (head + 1) * HEAD_DIM)
+                    piece = mixed[inner, head * tok_rows : (head + 1) * tok_rows]
+                    for image in range(own_count):
+                        total[image, outer] += piece * weights[image]
+
+    def step(number, carry):
+        layer = layer_at(number, z)
+        arrived(index(layer, y, 1 - core))
+        attend(layer, y)
+        across = index(layer, 1 - y, core)
+        arrived(across)
+        begin(across, SIBLING, sibling)
+
+        @pl.when(number < LAYERS - 1)
+        def _():
+            later = layer_at(number + 1, z)
+            arrived(index(later, y, core))
+            pass_on(later, begin)
+
+        arrived(index(layer, 1 - y, 1 - core))
+        attend(layer, 1 - y)
+        return carry
+
+    lax.fori_loop(0, LAYERS, step, 0)
+
+    for image in range(own_count):
+        context = (total[image] / counts_ref[image].astype(jnp.float32)).T.astype(jnp.bfloat16)
+        added = jnp.dot(context, w_out_ref[...], preferred_element_type=jnp.float32)
+        mixed_ref[image] = (tokens_ref[image].astype(jnp.float32) + added).astype(jnp.bfloat16)
+
+    def settle(number, carry):
+        layer = layer_at(number, z)
+        pass_on(layer, finish)
+        finish(index(layer, 1 - y, core), SIBLING, sibling)
+        return carry
+
+    lax.fori_loop(0, LAYERS, settle, 0)
+
+
+def fused(tokens, partners, counts, gain_query, gain_memory, w_query, w_key, w_value, w_out):
+    own_count, tok_rows, width = tokens.shape
+    peer_count = lax.axis_size("img")
+    vmem = pl.BlockSpec(memory_space=pltpu.VMEM)
+    smem = pl.BlockSpec(memory_space=pltpu.SMEM)
+    return pl.pallas_call(
+        fused_kernel,
+        out_shape=jax.ShapeDtypeStruct(tokens.shape, jnp.bfloat16),
+        in_specs=[vmem, smem, smem] + [vmem] * 6,
+        out_specs=vmem,
+        scratch_shapes=[
+            pltpu.VMEM((peer_count, own_count, tok_rows, width), jnp.bfloat16),
+            pltpu.VMEM((own_count, width // 128, 128, 2 * tok_rows), jnp.bfloat16),
+            pltpu.VMEM((width, width), jnp.bfloat16),
+            pltpu.VMEM((2 * tok_rows, width), jnp.bfloat16),
+            pltpu.VMEM((width, 2 * tok_rows), jnp.bfloat16),
+            pltpu.VMEM((own_count, width, tok_rows), jnp.float32),
+            pltpu.SemaphoreType.DMA((peer_count, 4)),
+            pltpu.SemaphoreType.DMA((peer_count,)),
+        ],
+        compiler_params=pltpu.CompilerParams(
+            collective_id=0, has_side_effects=True, vmem_limit_bytes=48 * 1024 * 1024
+        ),
+    )(
+        tokens,
+        partners,
+        counts,
+        gain_query.reshape(1, -1),
+        gain_memory.reshape(1, -1),
+        w_query,
+        w_key,
+        w_value,
+        w_out,
+    )
+
+
+def shards(tokens, partners, *params):
+    own_count, tok_rows, _ = tokens.shape
+    gathers = lax.axis_size("img") == 4 * LAYERS and own_count * partners.shape[1] >= 4 * LAYERS
+    if gathers and tok_rows == 128 and HEAD_DIM == 64 and own_count == 2:
+        return fused(tokens, partners, *params)
+    return exchange(tokens, partners, *params)
+
+
 def solution(mesh):
     placed = (
         P(("groups", "img"), None, None),

time: 161 us -> 65 us (0.40)
  the two profiles are of different devices: /device:TPU:13 before, /device:TPU:5 now
where the time goes in v1:
time: 65 us; the launch traced here: 64.6 us
  Pallas kernels  55 us (85%)
  local copies, waits for them, and re-layouts  9.53 us (15%)
    pallas_call x1, Pallas kernels, fused(): pl.pallas_call(fused_kernel, out_shape=jax.ShapeDtypeStruct(tokens.shape,...  55 us
    unnamed x15, local copies, waits for them, and re-layouts  8.16 us

profile of v1, /device:TPU:5, one launch (start us, length us, event | category | flops | bytes accessed | tf_op | source)
XLA Modules:
  0.0 64.6 jit_solution(1439674999745831146)
XLA Ops:
  0.0 0.7 %reshape.6.gain_query_ref = f32[1,768]{1,0:T(1,128)S(1)} reshape(f32[768]{0:T(1024)} %param.12) | data formatting | bytes 6144 | tf_op jit(solution)/shard_map/reshape | solution.py:338
  0.7 0.7 %reshape.7.gain_memory_ref = f32[1,768]{1,0:T(1,128)S(1)} reshape(f32[768]{0:T(1024)} %param.13) | data formatting | bytes 6144 | tf_op jit(solution)/shard_map/reshape | solution.py:339
  1.4 0.0 copy-start
  1.4 1.3 %copy-done = bf16[768,768]{1,0:T(8,128)(2,1)S(1)} copy-done((bf16[768,768]{1,0:T(8,128)(2,1)S(1)}, bf16[768,768]{1,0:T(8,128)(2,1)}, u32[]{:S(2)}) %copy-start) | copy-done | bytes 1179672
  2.7 0.0 copy-start.1
  2.7 1.3 %copy-done.1 = bf16[768,768]{1,0:T(8,128)(2,1)S(1)} copy-done((bf16[768,768]{1,0:T(8,128)(2,1)S(1)}, bf16[768,768]{1,0:T(8,128)(2,1)}, u32[]{:S(2)}) %copy-start.1) | copy-done | bytes 1179672
  3.9 0.0 copy-start.2
  3.9 1.3 %copy-done.2 = bf16[768,768]{1,0:T(8,128)(2,1)S(1)} copy-done((bf16[768,768]{1,0:T(8,128)(2,1)S(1)}, bf16[768,768]{1,0:T(8,128)(2,1)}, u32[]{:S(2)}) %copy-start.2) | copy-done | bytes 1179672
  5.2 0.0 copy-start.3
  5.2 1.3 %copy-done.3 = bf16[768,768]{1,0:T(8,128)(2,1)S(1)} copy-done((bf16[768,768]{1,0:T(8,128)(2,1)S(1)}, bf16[768,768]{1,0:T(8,128)(2,1)}, u32[]{:S(2)}) %copy-start.3) | copy-done | bytes 1179672
  6.5 0.0 copy-start.4
  6.5 1.0 %copy-done.4 = bf16[2,128,768]{2,1,0:T(8,128)(2,1)S(1)} copy-done((bf16[2,128,768]{2,1,0:T(8,128)(2,1)S(1)}, bf16[2,128,768]{2,1,0:T(8,128)(2,1)}, u32[]{:S(2)}) %copy-start.4) | copy-done | bytes 393240
  7.5 0.0 copy-start.5
  7.5 0.7 %copy-done.5 = s32[2,8]{1,0:T(2,128)S(1)} copy-done((s32[2,8]{1,0:T(2,128)S(1)}, s32[2,8]{1,0:T(2,128)}, u32[]{:S(2)}) %copy-start.5) | copy-done | bytes 88
  8.1 0.0 copy-start.6
  8.1 0.7 %copy-done.6 = s32[2]{0:T(128)S(1)} copy-done((s32[2]{0:T(128)S(1)}, s32[2]{0:T(128)}, u32[]{:S(2)}) %copy-start.6) | copy-done | bytes 32
  8.8 55.0 %shard_map.91 = bf16[2,128,768]{2,1,0:T(8,128)(2,1)S(1)} custom-call(bf16[2,128,768]{2,1,0:T(8,128)(2,1)S(1)} %copy-done.4, s32[2,8]{1,0:T(2,128)S(1)} %copy-done.5, s32[2]{0:T(128)S(1)} %copy-done.6, f32[1,768]{1,0:T(1,128)S(1)} %reshape.6.gain_query_ref, f32[1,768]{1,0:T(1,128)S(1)} %reshape.7.gain_memory_ref, bf16[768,768]{1,0:T(8,128)(2,1)S(1)} %copy-done, ...), custom_call_target="tpu_custom_call" | custom-call | tf_op jit(solution)/shard_map/pallas_call | solution.py:316
  63.8 0.7 %copy.11 = bf16[2,128,768]{2,1,0:T(8,128)(2,1)} copy(bf16[2,128,768]{2,1,0:T(8,128)(2,1)S(1)} %shard_map.91) | data formatting | bytes 786432
Async XLA Ops:
  1.4 1.3 %copy-start = (bf16[768,768]{1,0:T(8,128)(2,1)S(1)}, bf16[768,768]{1,0:T(8,128)(2,1)}, u32[]{:S(2)}) copy-start(bf16[768,768]{1,0:T(8,128)(2,1)} %w_query_ref.1) | copy-start | bytes 3538948
  2.7 1.3 %copy-start.1 = (bf16[768,768]{1,0:T(8,128)(2,1)S(1)}, bf16[768,768]{1,0:T(8,128)(2,1)}, u32[]{:S(2)}) copy-start(bf16[768,768]{1,0:T(8,128)(2,1)} %w_key_ref.1) | copy-start | bytes 3538948
  3.9 1.3 %copy-start.2 = (bf16[768,768]{1,0:T(8,128)(2,1)S(1)}, bf16[768,768]{1,0:T(8,128)(2,1)}, u32[]{:S(2)}) copy-start(bf16[768,768]{1,0:T(8,128)(2,1)} %w_value_ref.1) | copy-start | bytes 3538948
  5.2 1.3 %copy-start.3 = (bf16[768,768]{1,0:T(8,128)(2,1)S(1)}, bf16[768,768]{1,0:T(8,128)(2,1)}, u32[]{:S(2)}) copy-start(bf16[768,768]{1,0:T(8,128)(2,1)} %w_out_ref.1) | copy-start | bytes 3538948
  6.5 1.0 %copy-start.4 = (bf16[2,128,768]{2,1,0:T(8,128)(2,1)S(1)}, bf16[2,128,768]{2,1,0:T(8,128)(2,1)}, u32[]{:S(2)}) copy-start(bf16[2,128,768]{2,1,0:T(8,128)(2,1)} %tokens_ref.1) | copy-start | bytes 1179652
  7.5 0.7 %copy-start.5 = (s32[2,8]{1,0:T(2,128)S(1)}, s32[2,8]{1,0:T(2,128)}, u32[]{:S(2)}) copy-start(s32[2,8]{1,0:T(2,128)} %partners_ref.1) | copy-start | bytes 196
  8.1 0.7 %copy-start.6 = (s32[2]{0:T(128)S(1)}, s32[2]{0:T(128)}, u32[]{:S(2)}) copy-start(s32[2]{0:T(128)} %counts_ref.1) | copy-start | bytes 28

commit v2 on v1

--- a/solution.py
+++ b/solution.py
@@ -112,25 +112,28 @@
 
 
 def fused_kernel(
-    tokens_ref,
-    partners_ref,
-    counts_ref,
-    gain_query_ref,
-    gain_memory_ref,
-    w_query_ref,
-    w_key_ref,
-    w_value_ref,
-    w_out_ref,
-    mixed_ref,
-    held,
-    block_q,
-    w_turned,
-    keys_ref,
-    values_ref,
-    total,
-    send_sem,
-    recv_sem,
+    *refs,
 ):
+    sources, (mixed_ref,) = refs[:9], refs[9:10]
+    landed, load_sem = refs[10:19], refs[19]
+    (
+        tokens_ref,
+        partners_ref,
+        counts_ref,
+        gain_query_ref,
+        gain_memory_ref,
+        w_query_ref,
+        w_key_ref,
+        w_value_ref,
+        w_out_ref,
+    ) = landed
+    held, block_q, w_turned, keys_ref, values_ref, total, send_sem, recv_sem = refs[20:]
+    loads = [
+        pltpu.make_async_copy(source, place, load_sem.at[number])
+        for number, (source, place) in enumerate(zip(sources, landed))
+    ]
+    for number in (0, 4, 3, 5, 7, 6, 1, 2, 8):
+        loads[number].start()
     own_count, tok_rows, width = tokens_ref.shape
     listed = partners_ref.shape[1]
     pairs = width // 128
@@ -177,12 +180,14 @@
     def _():
         greet(down)
 
+    loads[0].wait()
+    loads[4].wait()
     rows = tokens_ref[...].reshape(own_count * tok_rows, width).astype(jnp.float32)
     center = rows - jnp.mean(rows, axis=-1, keepdims=True)
     spread = jnp.mean(center * center, axis=-1, keepdims=True)
     unit = center * lax.rsqrt(spread + 1e-06)
     held[me] = (
-        (unit * gain_memory_ref[...]).astype(jnp.bfloat16).reshape(own_count, tok_rows, width)
+        (unit * gain_memory_ref[...].reshape(1, width)).astype(jnp.bfloat16).reshape(own_count, tok_rows, width)
     )
 
     pl.semaphore_wait(barrier, 3 + (z + LAYERS - 2) // (LAYERS - 1) - z // (LAYERS - 1))
@@ -209,7 +214,9 @@
 
     pass_on(z, begin)
 
-    normed_query = (unit * gain_query_ref[...]).astype(jnp.bfloat16)
+    loads[3].wait()
+    loads[5].wait()
+    normed_query = (unit * gain_query_ref[...].reshape(1, width)).astype(jnp.bfloat16)
     w_turned[...] = w_query_ref[...].T
     queries = lax.dot_general(
         w_turned[...], normed_query, (((1,), (1,)), ((), ())), preferred_element_type=jnp.float32
@@ -223,7 +230,11 @@
             upper = jnp.concatenate([both[:HEAD_DIM], blank], axis=1)
             lower = jnp.concatenate([blank, both[HEAD_DIM:]], axis=1)
             block_q[image, pair] = jnp.concatenate([upper, lower], axis=0)
+    loads[7].wait()
     w_turned[...] = w_value_ref[...].T
+    loads[6].wait()
+    loads[1].wait()
+    loads[2].wait()
     total[...] = jnp.zeros_like(total)
 
     def pair_of(owner):
@@ -294,6 +305,7 @@
 
     lax.fori_loop(0, LAYERS, step, 0)
 
+    loads[8].wait()
     for image in range(own_count):
         context = (total[image] / counts_ref[image].astype(jnp.float32)).T.astype(jnp.bfloat16)
         added = jnp.dot(context, w_out_ref[...], preferred_element_type=jnp.float32)
@@ -311,14 +323,18 @@
 def fused(tokens, partners, counts, gain_query, gain_memory, w_query, w_key, w_value, w_out):
     own_count, tok_rows, width = tokens.shape
     peer_count = lax.axis_size("img")
-    vmem = pl.BlockSpec(memory_space=pltpu.VMEM)
-    smem = pl.BlockSpec(memory_space=pltpu.SMEM)
+    operands = (
+        tokens, partners, counts, gain_query, gain_memory, w_query, w_key, w_value, w_out
+    )
+    spaces = [pltpu.VMEM, pltpu.SMEM, pltpu.SMEM] + [pltpu.VMEM] * 6
     return pl.pallas_call(
         fused_kernel,
         out_shape=jax.ShapeDtypeStruct(tokens.shape, jnp.bfloat16),
-        in_specs=[vmem, smem, smem] + [vmem] * 6,
-        out_specs=vmem,
-        scratch_shapes=[
+        in_specs=[pl.BlockSpec(memory_space=pltpu.HBM)] * len(operands),
+        out_specs=pl.BlockSpec(memory_space=pltpu.VMEM),
+        scratch_shapes=[space(x.shape, x.dtype) for space, x in zip(spaces, operands)]
+        + [
+            pltpu.SemaphoreType.DMA((len(operands),)),
             pltpu.VMEM((peer_count, own_count, tok_rows, width), jnp.bfloat16),
             pltpu.VMEM((own_count, width // 128, 128, 2 * tok_rows), jnp.bfloat16),
             pltpu.VMEM((width, width), jnp.bfloat16),
@@ -329,19 +345,9 @@
             pltpu.SemaphoreType.DMA((peer_count,)),
         ],
         compiler_params=pltpu.CompilerParams(
-            collective_id=0, has_side_effects=True, vmem_limit_bytes=48 * 1024 * 1024
+            collective_id=0, has_side_effects=True, vmem_limit_bytes=63 * 1024 * 1024
         ),
-    )(
-        tokens,
-        partners,
-        counts,
-        gain_query.reshape(1, -1),
-        gain_memory.reshape(1, -1),
-        w_query,
-        w_key,
-        w_value,
-        w_out,
-    )
+    )(*operands)
 
 
 def shards(tokens, partners, *params):

time: 65 us -> 57.4 us (0.88)
  local copies, waits for them, and re-layouts: 9.53 us -> 1.77 us
    unnamed x15 -> x1, local copies, waits for them, and re-layouts: 8.16 us -> 1.77 us
    reshape x2 -> x0, local copies, waits for them, and re-layouts: 1.38 us -> none  [the longest x1 0.69 us: fused(): gain_memory.reshape(1, -1)]
where the time goes in v2:
time: 57.4 us; the launch traced here: 57.3 us
  Pallas kernels  55.5 us (97%)
  local copies, waits for them, and re-layouts  1.77 us (3%)
    pallas_call x1, Pallas kernels, fused(): pl.pallas_call(fused_kernel, out_shape=jax.ShapeDtypeStruct(tokens.shape,...  55.5 us
    unnamed x1, local copies, waits for them, and re-layouts  1.77 us

profile of v2, /device:TPU:5, one launch (start us, length us, event | category | flops | bytes accessed | tf_op | source)
XLA Modules:
  0.0 57.3 jit_solution(8995411899834578097)
XLA Ops:
  0.0 55.5 %shard_map.91 = bf16[2,128,768]{2,1,0:T(8,128)(2,1)} custom-call(bf16[2,128,768]{2,1,0:T(8,128)(2,1)} %refs_0_.1, s32[2,8]{1,0:T(2,128)} %refs_1_.1, s32[2]{0:T(128)} %refs_2_.1, f32[768]{0:T(1024)} %refs_3_.1, f32[768]{0:T(1024)} %refs_4_.1, bf16[768,768]{1,0:T(8,128)(2,1)} %refs_5_.1, bf16[768,768]{1,0:T(8,128)(2,1)} %refs_6_.1, bf16[768,768]{1,0:T(8,128)(2,1)} %refs_7_.1, ...), custom_call_target="tpu_custom_call" | custom-call | tf_op jit(solution)/shard_map/pallas_call | solution.py:330
  55.5 1.8 %copy.11 = bf16[2,128,768]{2,1,0:T(8,128)(2,1)} copy(bf16[2,128,768]{2,1,0:T(8,128)(2,1)} %shard_map.91) | data formatting | bytes 786432
